TPU v7x, 32 devices: a whole 2x2x4 slice. The times are simulated.
32 devices in a mesh: fsdp: 8 (over z, x), tp: 4 (over y, core).
Axes of the slice: x: 2, y: 2, z: 4, core: 2. Of those that a mesh axis runs over, the one named last changes fastest.
Arguments:
- inputs: bfloat16 [32768, 512], P(('fsdp', 'tp')), may hold values from -6 to 6
- segments: int32 [8, 4096], P('fsdp', 'tp'), may hold values from 0 to 20, as said below
- out_grad: bfloat16 [32768, 512], P(('fsdp', 'tp')), may hold values from -6 to 6
- first_gain: bfloat16 [512], replicated, may hold values from 0.5 to 1.5
- first_shift: bfloat16 [512], replicated, may hold values from -3 to 3
- qkv_weight: bfloat16 [512, 3, 512], P('fsdp', None, 'tp'), may hold values from -0.375 to 0.375
- qv_bias: bfloat16 [2, 512], replicated, may hold values from -3 to 3
- out_weight: bfloat16 [512, 512], P('tp', 'fsdp'), may hold values from -1 to 1
- out_bias: bfloat16 [512], replicated, may hold values from -3 to 3
- second_gain: bfloat16 [512], replicated, may hold values from 0.5 to 1.5
- second_shift: bfloat16 [512], replicated, may hold values from -3 to 3
- fc_weight: bfloat16 [512, 2048], P('fsdp', 'tp'), may hold values from -0.25 to 0.25
- fc_bias: bfloat16 [2048], replicated, may hold values from -3 to 3
- proj_weight: bfloat16 [2048, 512], P('tp', 'fsdp'), may hold values from -0.125 to 0.125
- proj_bias: bfloat16 [512], replicated, may hold values from -3 to 3
Outputs:
- layer_out: bfloat16 [32768, 512], P(('fsdp', 'tp'))
- input_grad: bfloat16 [32768, 512], P(('fsdp', 'tp'))
- first_gain_grad: float32 [512], replicated
- first_shift_grad: float32 [512], replicated
- qkv_weight_grad: float32 [512, 3, 512], P('fsdp', None, 'tp')
- qv_bias_grad: float32 [2, 512], replicated
- out_weight_grad: float32 [512, 512], P('tp', 'fsdp')
- out_bias_grad: float32 [512], replicated
- second_gain_grad: float32 [512], replicated
- second_shift_grad: float32 [512], replicated
- fc_weight_grad: float32 [512, 2048], P('fsdp', 'tp')
- fc_bias_grad: float32 [2048], replicated
- proj_weight_grad: float32 [2048, 512], P('tp', 'fsdp')
- proj_bias_grad: float32 [512], replicated
Inputs may be any that keep to these rules, and one draw needn't show every extreme that they name: `segments`: along each sequence the numbers start at 1 and rise by one from document to document; each document has 200 to 2000 tokens, and in one sequence every document has exactly 200; 0 marks padding, which only follows the last whole document of a sequence.
All inputs are finite; a program needn't handle non-finite values.
Results may differ from a plain program's by a relative error of at most 0.018.
The roundings to bfloat16 on the way count: a program that leaves them out, or rounds other values in their place, can miss the bound.
Values may be sent and summed in bfloat16 or wider, within the bound.
A program may use at most 128 MiB of HBM per device.

v0:
```python
import jax
import jax.numpy as jnp
from jax import lax
from jax.sharding import PartitionSpec as P

HD = 64
FF = 2048
epsilon = 1e-05
gelu_slope = 1.702
masked_score = -1e30


def split_up(value, dim, peers):
    dims = value.shape
    pieces = value.reshape(*dims[:dim], peers, dims[dim] // peers, *dims[dim + 1 :])
    return jnp.moveaxis(pieces, dim, 0)


def sent_and_summed(value, axis, dim):
    pieces = split_up(value, dim, lax.axis_size(axis))
    arrived = lax.all_to_all(pieces, axis, split_axis=0, concat_axis=0, tiled=True)
    return arrived.astype(jnp.float32).sum(axis=0)


def layer_norm(values_in, gain_vec, shift_vec):
    mean_row = jnp.mean(values_in, axis=-1, keepdims=True)
    centred = values_in - mean_row
    inverse = lax.rsqrt(jnp.mean(centred * centred, axis=-1, keepdims=True) + epsilon)
    normed = centred * inverse
    return (normed * gain_vec + shift_vec, normed, inverse)


def norm_back(grad_out, normed, inverse, gain_vec):
    scaled = grad_out * gain_vec
    grad_in = inverse * (
        scaled
        - jnp.mean(scaled, axis=-1, keepdims=True)
        - normed * jnp.mean(scaled * normed, axis=-1, keepdims=True)
    )
    return (grad_in, jnp.sum(grad_out * normed, axis=0), jnp.sum(grad_out, axis=0))


def allowed(seg_query, pos_query, seg_key, pos_key):
    same_doc = seg_query[:, None] == seg_key[None, :]
    causal = pos_key[None, :] <= pos_query[:, None]
    living = (seg_query[:, None] != 0) | (pos_key[None, :] == pos_query[:, None])
    return same_doc & causal & living


def attend(queries, keys_all, values_all, seg_all, block_rows):
    seq_rows, heads_here, head_size = queries.shape
    blocks = seq_rows // block_rows
    positions = jnp.arange(seq_rows, dtype=jnp.int32)
    scale_factor = head_size ** (-0.5)

    def one_block(pieces):
        q_blk, seg_blk, pos_blk = pieces
        scores = (
            jnp.einsum("qhe,khe->hqk", q_blk, keys_all, preferred_element_type=jnp.float32)
            * scale_factor
        )
        allowed_mask = allowed(seg_blk, pos_blk, seg_all, positions)
        scores = jnp.where(allowed_mask[None], scores, masked_score)
        row_max = jnp.max(scores, axis=-1, keepdims=True)
        exp_scores = jnp.exp(scores - row_max)
        row_sum = jnp.sum(exp_scores, axis=-1, keepdims=True)
        softmax_w = (exp_scores / row_sum).astype(jnp.bfloat16)
        block_out = jnp.einsum(
            "hqk,khe->qhe", softmax_w, values_all, preferred_element_type=jnp.float32
        )
        return (block_out, (row_max + jnp.log(row_sum))[..., 0])

    block_outs, log_norm = lax.map(
        one_block,
        (
            queries.reshape(blocks, block_rows, heads_here, head_size),
            seg_all.reshape(blocks, block_rows),
            positions.reshape(blocks, block_rows),
        ),
    )
    return (block_outs.reshape(seq_rows, heads_here, head_size), log_norm)


def attend_back(queries, keys_all, values_all, grad_out, raw_out, log_norm, seg_all, block_rows):
    seq_rows, heads_here, head_size = queries.shape
    blocks = seq_rows // block_rows
    positions = jnp.arange(seq_rows, dtype=jnp.int32)
    scale_factor = head_size ** (-0.5)
    row_dot = jnp.sum(grad_out.astype(jnp.float32) * raw_out, axis=-1)

    def one_block(running, pieces):
        grad_keys, grad_values = running
        q_blk, g_blk, dot_blk, norm_blk, seg_blk, pos_blk = pieces
        scores = (
            jnp.einsum("qhe,khe->hqk", q_blk, keys_all, preferred_element_type=jnp.float32)
            * scale_factor
        )
        allowed_mask = allowed(seg_blk, pos_blk, seg_all, positions)
        scores = jnp.where(allowed_mask[None], scores, masked_score)
        softmax_f = jnp.exp(scores - norm_blk[..., None])
        grad_soft = jnp.einsum(
            "qhe,khe->hqk", g_blk, values_all, preferred_element_type=jnp.float32
        )
        grad_scores = (softmax_f * (grad_soft - dot_blk.T[..., None]) * scale_factor).astype(
            jnp.bfloat16
        )
        grad_q = jnp.einsum(
            "hqk,khe->qhe", grad_scores, keys_all, preferred_element_type=jnp.float32
        )
        grad_keys = grad_keys + jnp.einsum(
            "hqk,qhe->khe", grad_scores, q_blk, preferred_element_type=jnp.float32
        )
        grad_values = grad_values + jnp.einsum(
            "hqk,qhe->khe",
            softmax_f.astype(jnp.bfloat16),
            g_blk,
            preferred_element_type=jnp.float32,
        )
        return ((grad_keys, grad_values), grad_q)

    zero_state = jnp.zeros((seq_rows, heads_here, head_size), jnp.float32)
    (grad_keys, grad_values), grad_queries = lax.scan(
        one_block,
        (zero_state, zero_state),
        (
            queries.reshape(blocks, block_rows, heads_here, head_size),
            grad_out.reshape(blocks, block_rows, heads_here, head_size),
            row_dot.reshape(blocks, block_rows, heads_here),
            log_norm,
            seg_all.reshape(blocks, block_rows),
            positions.reshape(blocks, block_rows),
        ),
    )
    return (grad_queries.reshape(seq_rows, heads_here, head_size), grad_keys, grad_values)


def local(
    inputs,
    segments,
    out_grad,
    first_gain,
    first_shift,
    qkv_weight,
    qv_bias,
    out_weight,
    out_bias,
    second_gain,
    second_shift,
    fc_weight,
    fc_bias,
    proj_weight,
    proj_bias,
):
    tp_index = lax.axis_index("tp")
    qkv_full, out_full, fc_full, proj_full = (
        lax.all_gather(qkv_weight, "fsdp", axis=0, tiled=True),
        lax.all_gather(out_weight, "fsdp", axis=1, tiled=True),
        lax.all_gather(fc_weight, "fsdp", axis=0, tiled=True),
        lax.all_gather(proj_weight, "fsdp", axis=1, tiled=True),
    )
    model_width = inputs.shape[1]
    head_cols = qkv_full.shape[2]
    hidden_cols = fc_full.shape[1]
    heads_here = head_cols // HD
    resid_in = inputs.astype(jnp.float32)
    normed_one, hat_one, inv_one = layer_norm(
        resid_in, first_gain.astype(jnp.float32), first_shift.astype(jnp.float32)
    )
    lowered_one = normed_one.astype(jnp.bfloat16)
    seq_normed, seg_rows = (
        lax.all_gather(lowered_one, "tp", axis=0, tiled=True),
        lax.all_gather(segments, "tp", axis=1, tiled=True),
    )
    seg_all = seg_rows[0]
    seq_rows = seq_normed.shape[0]
    block_rows = min(512, seq_rows)
    projected = jnp.einsum("sd,dje->sje", seq_normed, qkv_full, preferred_element_type=jnp.float32)
    bias_here = lax.dynamic_slice_in_dim(qv_bias, tp_index * head_cols, head_cols, 1).astype(
        jnp.float32
    )
    queries = (
        (projected[:, 0] + bias_here[0]).astype(jnp.bfloat16).reshape(seq_rows, heads_here, HD)
    )
    keys_all = projected[:, 1].astype(jnp.bfloat16).reshape(seq_rows, heads_here, HD)
    values_all = (
        (projected[:, 2] + bias_here[1]).astype(jnp.bfloat16).reshape(seq_rows, heads_here, HD)
    )
    live_rows = (seg_all != 0).astype(jnp.float32)
    raw_out, log_norm = attend(queries, keys_all, values_all, seg_all, block_rows)
    attn_low = (
        (raw_out * live_rows[:, None, None]).astype(jnp.bfloat16).reshape(seq_rows, head_cols)
    )
    attn_sum = lax.psum_scatter(
        jnp.dot(attn_low, out_full, preferred_element_type=jnp.float32).astype(jnp.bfloat16),
        "tp",
        scatter_dimension=0,
        tiled=True,
    ).astype(jnp.float32)
    hidden = resid_in + attn_sum + out_bias.astype(jnp.float32)
    normed_two, hat_two, inv_two = layer_norm(
        hidden, second_gain.astype(jnp.float32), second_shift.astype(jnp.float32)
    )
    lowered_two = normed_two.astype(jnp.bfloat16)
    mlp_in = lax.all_gather(lowered_two, "tp", axis=0, tiled=True)
    fc_bias_here = lax.dynamic_slice_in_dim(fc_bias, tp_index * hidden_cols, hidden_cols, 0)
    pre_act = jnp.dot(mlp_in, fc_full, preferred_element_type=jnp.float32) + fc_bias_here.astype(
        jnp.float32
    )
    sigmoid_pre = jax.nn.sigmoid(gelu_slope * pre_act)
    act_low = (pre_act * sigmoid_pre).astype(jnp.bfloat16)
    mlp_sum = lax.psum_scatter(
        jnp.dot(act_low, proj_full, preferred_element_type=jnp.float32).astype(jnp.bfloat16),
        "tp",
        scatter_dimension=0,
        tiled=True,
    ).astype(jnp.float32)
    grad_rows = lax.all_gather(out_grad, "tp", axis=0, tiled=True)
    layer_out = (hidden + mlp_sum + proj_bias.astype(jnp.float32)).astype(jnp.bfloat16)
    proj_grad = jnp.einsum("sf,sd->fd", act_low, grad_rows, preferred_element_type=jnp.float32)
    grad_act = jnp.einsum("sd,fd->sf", grad_rows, proj_full, preferred_element_type=jnp.float32)
    grad_pre = grad_act * (sigmoid_pre + gelu_slope * pre_act * sigmoid_pre * (1.0 - sigmoid_pre))
    grad_pre_low = grad_pre.astype(jnp.bfloat16)
    fc_grad = jnp.einsum("sd,sf->df", mlp_in, grad_pre_low, preferred_element_type=jnp.float32)
    fc_bias_part = jnp.sum(grad_pre_low.astype(jnp.float32), axis=0)
    grad_normed_two = lax.psum_scatter(
        jnp.einsum("sf,df->sd", grad_pre_low, fc_full, preferred_element_type=jnp.float32).astype(
            jnp.bfloat16
        ),
        "tp",
        scatter_dimension=0,
        tiled=True,
    ).astype(jnp.float32)
    fc_bias_full = lax.dynamic_update_slice_in_dim(
        jnp.zeros((FF,), jnp.float32), fc_bias_part, tp_index * hidden_cols, 0
    )
    resid_grad = out_grad.astype(jnp.float32)
    grad_hidden_ln, second_gain_part, second_shift_part = norm_back(
        grad_normed_two, hat_two, inv_two, second_gain.astype(jnp.float32)
    )
    grad_hidden = resid_grad + grad_hidden_ln
    grad_hidden_low = grad_hidden.astype(jnp.bfloat16)
    out_bias_part = jnp.sum(grad_hidden_low.astype(jnp.float32), axis=0)
    proj_bias_part = jnp.sum(resid_grad, axis=0)
    seq_grad = lax.all_gather(grad_hidden_low, "tp", axis=0, tiled=True)
    out_w_grad = jnp.einsum("sc,sd->cd", attn_low, seq_grad, preferred_element_type=jnp.float32)
    grad_attn = jnp.einsum("sd,cd->sc", seq_grad, out_full, preferred_element_type=jnp.float32)
    grad_attn_low = (
        grad_attn.astype(jnp.bfloat16).reshape(seq_rows, heads_here, HD)
        * live_rows.astype(jnp.bfloat16)[:, None, None]
    )
    grad_q, grad_k, grad_v = attend_back(
        queries, keys_all, values_all, grad_attn_low, raw_out, log_norm, seg_all, block_rows
    )
    grad_qkv = (
        jnp.stack([grad_q, grad_k, grad_v], axis=1)
        .astype(jnp.bfloat16)
        .reshape(seq_rows, 3, head_cols)
    )
    qkv_w_grad = jnp.einsum("sd,sje->dje", seq_normed, grad_qkv, preferred_element_type=jnp.float32)
    qv_part = jnp.sum(grad_qkv[:, 0::2].astype(jnp.float32), axis=0)
    grad_normed_one = lax.psum_scatter(
        jnp.einsum("sje,dje->sd", grad_qkv, qkv_full, preferred_element_type=jnp.float32).astype(
            jnp.bfloat16
        ),
        "tp",
        scatter_dimension=0,
        tiled=True,
    ).astype(jnp.float32)
    qv_full = lax.dynamic_update_slice_in_dim(
        jnp.zeros((2, model_width), jnp.float32), qv_part, tp_index * head_cols, 1
    )
    grad_in_ln, first_gain_part, first_shift_part = norm_back(
        grad_normed_one, hat_one, inv_one, first_gain.astype(jnp.float32)
    )
    input_grad = (grad_hidden + grad_in_ln).astype(jnp.bfloat16)
    qkv_w_grad, out_w_grad, fc_grad, proj_grad = (
        sent_and_summed(qkv_w_grad.astype(jnp.bfloat16), "fsdp", 0),
        sent_and_summed(out_w_grad.astype(jnp.bfloat16), "fsdp", 1),
        sent_and_summed(fc_grad.astype(jnp.bfloat16), "fsdp", 0),
        sent_and_summed(proj_grad.astype(jnp.bfloat16), "fsdp", 1),
    )
    (
        first_gain_grad,
        first_shift_grad,
        qv_bias_grad,
        out_bias_grad,
        second_gain_grad,
        second_shift_grad,
        fc_bias_grad,
        proj_bias_grad,
    ) = lax.psum(
        (
            first_gain_part,
            first_shift_part,
            qv_full,
            out_bias_part,
            second_gain_part,
            second_shift_part,
            fc_bias_full,
            proj_bias_part,
        ),
        ("fsdp", "tp"),
    )
    return (
        layer_out,
        input_grad,
        first_gain_grad,
        first_shift_grad,
        qkv_w_grad,
        qv_bias_grad,
        out_w_grad,
        out_bias_grad,
        second_gain_grad,
        second_shift_grad,
        fc_grad,
        fc_bias_grad,
        proj_grad,
        proj_bias_grad,
    )


def solution(mesh):
    return jax.shard_map(
        local,
        mesh=mesh,
        in_specs=(
            P(("fsdp", "tp"), None),
            P("fsdp", "tp"),
            P(("fsdp", "tp"), None),
            P(),
            P(),
            P("fsdp", None, "tp"),
            P(),
            P("tp", "fsdp"),
            P(),
            P(),
            P(),
            P("fsdp", "tp"),
            P(),
            P("tp", "fsdp"),
            P(),
        ),
        out_specs=(
            P(("fsdp", "tp"), None),
            P(("fsdp", "tp"), None),
            P(),
            P(),
            P("fsdp", None, "tp"),
            P(),
            P("tp", "fsdp"),
            P(),
            P(),
            P(),
            P("fsdp", "tp"),
            P(),
            P("tp", "fsdp"),
            P(),
        ),
        check_vma=False,
    )
```

profile of v0, /device:TPU:0, one launch (start us, length us, event | category | flops | bytes accessed | tf_op | source)
XLA Modules:
  0.0 1055.5 jit_solution(14751792335652611730)
XLA Ops:
  23.5 33.3 %all_gather.30 = bf16[128,512]{0,1:T(8,128)(2,1)} all-gather(bf16[128,64]{0,1:T(8,128)(2,1)S(1)} %copy-done.28), channel_id=1, replica_groups=mesh['fsdp'=8,'tp'=4] {'fsdp'}, dimensions={1}, use_global_device_ids=true | all-gather | bytes 147456 | tf_op jit(solution)/shard_map/all_gather | solution.py:157
  56.8 31.0 %all_gather.29 = bf16[512,3,128]{2,0,1:T(8,128)(2,1)S(1)} all-gather(bf16[64,3,128]{2,0,1:T(8,128)(2,1)S(1)} %copy-done.26), channel_id=1, replica_groups=mesh['fsdp'=8,'tp'=4] {'fsdp'}, dimensions={0}, use_global_device_ids=true | all-gather | bytes 442368 | tf_op jit(solution)/shard_map/all_gather | solution.py:156
  97.2 209.4 %while.30 = (s32[]{:T(128)}, f32[8,512,2,64]{1,0,3,2:T(8,128)}, f32[8,2,512]{2,1,0:T(2,128)S(1)}, s32[8,512]{1,0:T(8,128)S(1)}, s32[1,4096]{1,0:T(1,128)S(1)}, /...) while((s32[]{:T(128)}, f32[8,512,2,64]{1,0,3,2:T(8,128)}, ...), condition=%wide.region_5.6_spmd.clone.clone, body=%wide.region_2.5_spmd.clone.clone.sunk | while | flops 1136655872 | bytes 62323844 | solution.py:73
  315.6 45.1 %reduce-scatter.5.cloned.1.call-done = bf16[1024,512]{1,0:T(8,128)(2,1)} async-done(((bf16[4096,512]{1,0:T(8,128)(2,1)}), bf16[1024,512]{1,0:T(8,128)(2,1)}) %reduce-scatter.5.cloned.1.call-update) | async-done | bytes 1048592 | tf_op jit(solution)/shard_map/reduce_scatter | solution.py:193
  367.3 33.5 %all_gather.32 = bf16[512,512]{1,0:T(8,128)(2,1)} all-gather(bf16[64,512]{1,0:T(8,128)(2,1)S(1)} %copy-done.24), channel_id=1, replica_groups=mesh['fsdp'=8,'tp'=4] {'fsdp'}, dimensions={0}, use_global_device_ids=true | all-gather | bytes 589824 | tf_op jit(solution)/shard_map/all_gather | solution.py:158
  400.8 33.5 %all_gather.33 = bf16[512,512]{0,1:T(8,128)(2,1)} all-gather(bf16[512,64]{0,1:T(8,128)(2,1)S(1)} %copy-done.25), channel_id=1, replica_groups=mesh['fsdp'=8,'tp'=4] {'fsdp'}, dimensions={1}, use_global_device_ids=true | all-gather | bytes 589824 | tf_op jit(solution)/shard_map/all_gather | solution.py:159
  434.3 10.4 multiply_convert_fusion.2
  444.7 9.8 convert_reduce_fusion
  468.5 37.5 %reduce-scatter.9.cloned.1.call-done = bf16[1024,512]{1,0:T(8,128)(2,1)} async-done(((bf16[4096,512]{1,0:T(8,128)(2,1)}), bf16[1024,512]{1,0:T(8,128)(2,1)}) %reduce-scatter.9.cloned.1.call-update) | async-done | bytes 1048592 | tf_op jit(solution)/shard_map/reduce_scatter | solution.py:225
  509.2 43.7 %reduce-scatter.7.cloned.1.call-done = bf16[1024,512]{1,0:T(8,128)(2,1)} async-done(((bf16[4096,512]{1,0:T(8,128)(2,1)}), bf16[1024,512]{1,0:T(8,128)(2,1)}) %reduce-scatter.7.cloned.1.call-update) | async-done | bytes 1048592 | tf_op jit(solution)/shard_map/reduce_scatter | solution.py:211
  557.9 34.5 %all-gather.11.cloned.1.call-done = bf16[4096,512]{1,0:T(8,128)(2,1)} async-done(((bf16[1024,512]{1,0:T(8,128)(2,1)}), bf16[4096,512]{1,0:T(8,128)(2,1)}) %all-gather.11.cloned.1.call-update) | async-done | bytes 4194320 | tf_op jit(solution)/shard_map/all_gather | solution.py:244
  602.7 300.8 %while.31 = (s32[]{:T(128)}, f32[4096,2,64]{0,2,1:T(8,128)S(1)}, f32[4096,2,64]{0,2,1:T(8,128)}, bf16[8,512,2,64]{1,3,2,0:T(8,128)(2,1)}, bf16[8,512,2,64]{1,3,2...) while((s32[]{:T(128)}, f32[4096,2,64]{0,2,1:T(8,128)S(1)}, ...), condition=%wide.region_15.16_spmd.clone.clone, body=%wide.region_14.15_spmd.clone.clone.sunk | while | flops 2745172480 | bytes 161287376 | solution.py:122
  623.5 10.5 multiply_convert_fusion.7
  661.1 10.5 multiply_convert_fusion.7
  698.6 10.5 multiply_convert_fusion.7
  736.2 10.5 multiply_convert_fusion.7
  773.8 10.5 multiply_convert_fusion.7
  811.4 10.5 multiply_convert_fusion.7
  849.0 10.5 multiply_convert_fusion.7
  886.6 10.5 multiply_convert_fusion.7
  942.9 8.3 all-to-all-done.3
  957.4 12.2 %all-to-all-done.2 = bf16[8,64,512]{2,1,0:T(8,128)(2,1)} async-done(((bf16[8,64,512]{2,1,0:T(8,128)(2,1)}), bf16[8,64,512]{2,1,0:T(8,128)(2,1)}, u32[]{:S(2)}, u32[]{:S(2)}) %all-to-all-start.2) | async-done | bytes 524320 | tf_op jit(solution)/shard_map/all_to_all | solution.py:21
  995.2 7.6 all-to-all-done
  1006.0 39.5 %all-reduce = (f32[512]{0:T(512)}, f32[512]{0:T(512)}, f32[2,512]{1,0:T(2,128)}, f32[512]{0:T(512)}, f32[512]{0:T(512)}, /*index=5*/f32[512]{0:T(512)}, f32[2048]{0:T(1024)}, f32[512]{0:T(512)}) all-reduce(f32[512]{0:T(512)S(1)} %get-tuple-element.300, ...), channel_id=1, replica_groups=mesh['fsdp'=8,'tp'=4] {'fsdp','tp'}, use_global_device_ids=true, to_apply=%region_20.21 | all-reduce | flops 6144 | bytes 49152 | tf_op jit(solution)/shard_map/psum | solution.py:291
  (343 shorter events, 574.5 us)
Async XLA Ops:
  7.2 16.3 %copy-start.28 = (bf16[128,64]{0,1:T(8,128)(2,1)S(1)}, bf16[128,64]{0,1:T(8,128)(2,1)}, u32[]{:S(2)}) copy-start(bf16[128,64]{0,1:T(8,128)(2,1)} %param.26) | copy-start | bytes 49156
  7.2 49.6 %copy-start.26 = (bf16[64,3,128]{2,0,1:T(8,128)(2,1)S(1)}, bf16[64,3,128]{2,0,1:T(8,128)(2,1)}, u32[]{:S(2)}) copy-start(bf16[64,3,128]{2,0,1:T(8,128)(2,1)} %param.24) | copy-start | bytes 147460
  7.2 81.2 %all-gather.5.cloned.1.call-start = ((), (), s32[]{:S(2)}) async-start(), calls=%async_computation.8 | async-start | bytes 5242880 | tf_op jit(solution)/shard_map/all_gather | solution.py:171
  15.1 345.6 %reduce-scatter.5.cloned.1.call-start = ((), (), s32[]{:S(2)}) async-start(), calls=%async_computation.9 | async-start | bytes 5242880 | tf_op jit(solution)/shard_map/reduce_scatter | solution.py:193
  314.9 45.9 %copy-start.1 = (bf16[1024,512]{1,0:T(8,128)(2,1)S(1)}, bf16[1024,512]{1,0:T(8,128)(2,1)}, u32[]{:S(2)}) copy-start(bf16[1024,512]{1,0:T(8,128)(2,1)} %param.19) | copy-start | bytes 3145732
  314.9 119.4 %all-gather.7.cloned.1.call-start = ((), (), s32[]{:S(2)}) async-start(), calls=%async_computation.10 | async-start | bytes 5242880 | tf_op jit(solution)/shard_map/all_gather | solution.py:204
  364.3 36.5 %copy-start.25 = (bf16[512,64]{0,1:T(8,128)(2,1)S(1)}, bf16[512,64]{0,1:T(8,128)(2,1)}, u32[]{:S(2)}) copy-start(bf16[512,64]{0,1:T(8,128)(2,1)} %param.32) | copy-start | bytes 196612
  365.9 78.8 %all-gather.9.cloned.1.call-start = ((), (), s32[]{:S(2)}) async-start(), calls=%async_computation.12 | async-start | bytes 5242880 | tf_op jit(solution)/shard_map/all_gather | solution.py:217
  366.5 139.4 %reduce-scatter.9.cloned.1.call-start = ((), (), s32[]{:S(2)}) async-start(), calls=%async_computation.13 | async-start | bytes 5242880 | tf_op jit(solution)/shard_map/reduce_scatter | solution.py:225
  461.0 91.9 %reduce-scatter.7.cloned.1.call-start = ((), (), s32[]{:S(2)}) async-start(), calls=%async_computation.11 | async-start | bytes 5242880 | tf_op jit(solution)/shard_map/reduce_scatter | solution.py:211
  467.8 124.6 %all-gather.11.cloned.1.call-start = ((), (), s32[]{:S(2)}) async-start(), calls=%async_computation.14 | async-start | bytes 5242880 | tf_op jit(solution)/shard_map/all_gather | solution.py:244
  557.8 445.7 %reduce-scatter.11.cloned.1.call-start = ((), (), s32[]{:S(2)}) async-start(), calls=%async_computation.15 | async-start | bytes 5242880 | tf_op jit(solution)/shard_map/reduce_scatter | solution.py:261
  930.6 20.5 %all-to-all-start.3 = ((bf16[8,512,64]{1,2,0:T(8,128)(2,1)}), bf16[8,512,64]{1,2,0:T(8,128)(2,1)}, u32[]{:S(2)}, u32[]{:S(2)}) async-start(bf16[8,512,64]{1,2,0:T(8,128)(2,1)} %bitcast.13), calls=%async_computation.7 | async-start | bytes 1048576 | tf_op jit(solution)/shard_map/all_to_all | solution.py:21
  936.2 19.2 %copy-start.31 = (f32[512]{0:T(512)S(1)}, f32[512]{0:T(512)}, u32[]{:S(2)}) copy-start(f32[512]{0:T(512)} %get-tuple-element.377) | copy-start | bytes 6148
  936.2 35.2 %copy-start.19 = (f32[1,4096]{1,0:T(1,128)S(1)}, f32[1,4096]{1,0:T(1,128)}, u32[]{:S(2)}) copy-start(f32[1,4096]{1,0:T(1,128)} %compare_convert_fusion) | copy-start | bytes 49156
  942.9 28.5 %copy-start.4 = (f32[16,8,8,512]{3,1,2,0:T(8,128)S(1)}, f32[16,8,8,512]{3,1,2,0:T(8,128)}, u32[]{:S(2)}) copy-start(f32[16,8,8,512]{3,1,2,0:T(8,128)} %copy-done.3) | copy-start | bytes 6291460
  951.2 18.4 %all-to-all-start.2 = ((bf16[8,64,512]{2,1,0:T(8,128)(2,1)}), bf16[8,64,512]{2,1,0:T(8,128)(2,1)}, u32[]{:S(2)}, u32[]{:S(2)}) async-start(bf16[8,64,512]{2,1,0:T(8,128)(2,1)} %bitcast.175), calls=%async_computation.6 | async-start | bytes 1048576 | tf_op jit(solution)/shard_map/all_to_all | solution.py:21
  975.0 11.0 %all-to-all-start.1 = ((bf16[8,128,64]{1,2,0:T(8,128)(2,1)}), bf16[8,128,64]{1,2,0:T(8,128)(2,1)S(1)}, u32[]{:S(2)}, u32[]{:S(2)}) async-start(bf16[8,128,64]{1,2,0:T(8,128)(2,1)} %bitcast.10), calls=%async_computation.5 | async-start | bytes 262144 | tf_op jit(solution)/shard_map/all_to_all | solution.py:21
  978.7 13.0 %copy-start.11 = (bf16[4096,1,128]{2,0,1:T(8,128)(2,1)S(1)}, bf16[4096,1,128]{2,0,1:T(8,128)(2,1)}, u32[]{:S(2)}) copy-start(bf16[4096,1,128]{2,0,1:T(8,128)(2,1)} %copy-done.10) | copy-start | bytes 3145732
  986.7 16.1 %all-to-all-start = ((bf16[8,64,3,128]{3,1,2,0:T(8,128)(2,1)}), bf16[8,64,3,128]{3,1,2,0:T(8,128)(2,1)S(1)}, u32[]{:S(2)}, u32[]{:S(2)}) async-start(bf16[8,64,3,128]{3,1,2,0:T(8,128)(2,1)} %copy.57), calls=%async_computation.4 | async-start | bytes 786432 | tf_op jit(solution)/shard_map/all_to_all | solution.py:21
  991.7 11.8 %copy-start.2 = (bf16[1024,512]{1,0:T(8,128)(2,1)S(1)}, bf16[1024,512]{1,0:T(8,128)(2,1)}, u32[]{:S(2)}) copy-start(bf16[1024,512]{1,0:T(8,128)(2,1)} %param.19) | copy-start | bytes 3145732
  991.7 11.8 %copy-start.21 = (f32[1024]{0:T(1024)S(1)}, f32[1024]{0:T(1024)}, u32[]{:S(2)}) copy-start(f32[1024]{0:T(1024)} %copy-done.20) | copy-start | bytes 12292
  991.7 11.8 %copy-start.23 = (f32[1024]{0:T(1024)S(1)}, f32[1024]{0:T(1024)}, u32[]{:S(2)}) copy-start(f32[1024]{0:T(1024)} %copy-done.22) | copy-start | bytes 12292
  993.4 52.1 %copy-start.6 = (f32[1024,512]{1,0:T(8,128)S(1)}, f32[1024,512]{1,0:T(8,128)}, u32[]{:S(2)}) copy-start(f32[1024,512]{1,0:T(8,128)} %get-tuple-element.362) | copy-start | bytes 6291460
  (32 other events, 125.5 us)
Sparse Core Ops, SparseCore 0:
  15.2 37.1 all-gather.4
  315.0 45.6 reduce-scatter.4
  366.0 34.4 all-gather.6
  401.9 34.4 all-gather.8
  461.1 44.7 reduce-scatter.8
  508.3 44.5 reduce-scatter.6
  557.9 34.4 all-gather.10
  924.1 44.5 reduce-scatter.10
where the time goes:
time: 1060 us
  matrix products  373 us (35%)
  waiting for transfers between devices  191 us (18%)
  blocking collectives  177 us (17%)
  other arithmetic  147 us (14%)
  local copies, waits for them, and re-layouts  132 us (12%)
  starting transfers between devices  18.6 us (2%)
  between operations  15.2 us (1%)
    dot_general x8, matrix products, one_block(): jnp.einsum('qhe,khe->hqk', g_blk, values_all, preferred_element_type=jnp....  84.2 us
    and x16, other arithmetic, allowed(): return same_doc & causal & living  69.2 us
    dot_general x8, matrix products, one_block(): jnp.einsum('hqk,qhe->khe', softmax_f.astype(jnp.bfloat16), g_blk, preferr...  60.4 us
    dot_general x16, matrix products, one_block(): jnp.einsum('qhe,khe->hqk', q_blk, keys_all, preferred_element_type=jnp.fl...  56.1 us
    dot_general x8, matrix products, one_block(): jnp.einsum('hqk,khe->qhe', softmax_w, values_all, preferred_element_type=...  54.3 us
    dynamic_update_slice x16, local copies, waits for them, and re-layouts, attend(): lax.map(one_block, (queries.reshape(blocks, block_rows, heads_here, head_...  53 us
    while x16, local copies, waits for them, and re-layouts  45.6 us
    reduce_scatter x1, waiting for transfers between devices, local(): lax.psum_scatter(jnp.dot(attn_low, out_full, preferred_element_type=jnp.f...  45.1 us
  transfers between devices with their start and end apart: 12, of which 8 were waited for; matrix products, arithmetic and copies ran while one was open for 5% of the time, Pallas kernels for 0%

commit v1 on v0

--- a/solution.py
+++ b/solution.py
@@ -8,6 +8,12 @@
 epsilon = 1e-05
 gelu_slope = 1.702
 masked_score = -1e30
+
+
+def joined_along(blocks, dim):
+    blocks = jnp.moveaxis(blocks, 0, dim)
+    dims = blocks.shape
+    return blocks.reshape(*dims[:dim], dims[dim] * dims[dim + 1], *dims[dim + 2 :])
 
 
 def split_up(value, dim, peers):
@@ -241,7 +247,14 @@
     grad_hidden_low = grad_hidden.astype(jnp.bfloat16)
     out_bias_part = jnp.sum(grad_hidden_low.astype(jnp.float32), axis=0)
     proj_bias_part = jnp.sum(resid_grad, axis=0)
-    seq_grad = lax.all_gather(grad_hidden_low, "tp", axis=0, tiled=True)
+    size = lax.axis_size("tp")
+    forward = [(i, (i + 1) % size) for i in range(size)]
+    blocks_2 = [grad_hidden_low]
+    while len(blocks_2) < size:
+        blocks_2.append(lax.ppermute(blocks_2[-1], "tp", forward))
+    index = lax.axis_index("tp")
+    blocks_2 = jnp.stack(blocks_2)[(index - jnp.arange(size)) % size]
+    seq_grad = joined_along(blocks_2, 0)
     out_w_grad = jnp.einsum("sc,sd->cd", attn_low, seq_grad, preferred_element_type=jnp.float32)
     grad_attn = jnp.einsum("sd,cd->sc", seq_grad, out_full, preferred_element_type=jnp.float32)
     grad_attn_low = (

time: 1060 us -> 1030 us (0.972)
  local copies, waits for them, and re-layouts: 132 us -> 85.7 us
    dynamic_update_slice x16 -> x0, local copies, waits for them, and re-layouts: 53 us -> none  [attend(): lax.map(one_block, (queries.reshape(blocks, block_rows, heads_here, head_...]
    ppermute x0 -> x3, waiting for transfers between devices: none -> 41.4 us  [local(): blocks_2.append(lax.ppermute(blocks_2[-1], 'tp', forward))]
    all_gather x1 -> x0, waiting for transfers between devices: 34.5 us -> none  [local(): seq_grad = lax.all_gather(grad_hidden_low, 'tp', axis=0, tiled=True)]
    while x16 -> x17, local copies, waits for them, and re-layouts: 45.6 us -> 46.9 us
  transfers between devices with their start and end apart: 12 -> 14, of which waited for: 8 -> 10; matrix products, arithmetic and copies ran while one was open for 5% -> 6% of each run, Pallas kernels for 0% -> 0%
where the time goes in v1:
time: 1030 us; the launch traced here: 1020 us
  matrix products  380 us (37%)
  waiting for transfers between devices  192 us (19%)
  blocking collectives  177 us (17%)
  other arithmetic  154 us (15%)
  local copies, waits for them, and re-layouts  85.7 us (8%)
  starting transfers between devices  18 us (2%)
  between operations  15.1 us (1%)
    dot_general x8, matrix products, one_block(): jnp.einsum('qhe,khe->hqk', g_blk, values_all, preferred_element_type=jnp....  84.2 us
    and x16, other arithmetic, allowed(): return same_doc & causal & living  69.2 us
    dot_general x16, matrix products, one_block(): jnp.einsum('qhe,khe->hqk', q_blk, keys_all, preferred_element_type=jnp.fl...  63.3 us
    dot_general x8, matrix products, one_block(): jnp.einsum('hqk,qhe->khe', softmax_f.astype(jnp.bfloat16), g_blk, preferr...  60.4 us
    dot_general x8, matrix products, one_block(): jnp.einsum('hqk,khe->qhe', softmax_w, values_all, preferred_element_type=...  54.3 us
    while x16, local copies, waits for them, and re-layouts  45.6 us
    reduce_scatter x1, waiting for transfers between devices, local(): lax.psum_scatter(jnp.dot(attn_low, out_full, preferred_element_type=jnp.f...  45.1 us
    reduce_scatter x1, waiting for transfers between devices, local(): lax.psum_scatter(jnp.dot(act_low, proj_full, preferred_element_type=jnp.f...  43.7 us
  transfers between devices with their start and end apart: 14, of which 10 were waited for; matrix products, arithmetic and copies ran while one was open for 6% of the time, Pallas kernels for 0%

profile of v1, /device:TPU:0, one launch (start us, length us, event | category | flops | bytes accessed | tf_op | source)
XLA Modules:
  0.0 1024.3 jit_solution(2278450643396322352)
XLA Ops:
  23.5 33.3 %all_gather.27 = bf16[128,512]{0,1:T(8,128)(2,1)} all-gather(bf16[128,64]{0,1:T(8,128)(2,1)S(1)} %copy-done.30), channel_id=1, replica_groups=mesh['fsdp'=8,'tp'=4] {'fsdp'}, dimensions={1}, use_global_device_ids=true | all-gather | bytes 147456 | tf_op jit(solution)/shard_map/all_gather | solution.py:163
  56.8 31.0 %all_gather.26 = bf16[512,3,128]{2,0,1:T(8,128)(2,1)S(1)} all-gather(bf16[64,3,128]{2,0,1:T(8,128)(2,1)S(1)} %copy-done.28), channel_id=1, replica_groups=mesh['fsdp'=8,'tp'=4] {'fsdp'}, dimensions={0}, use_global_device_ids=true | all-gather | bytes 442368 | tf_op jit(solution)/shard_map/all_gather | solution.py:162
  98.2 163.7 %while.32 = (s32[]{:T(128)}, f32[8,512,2,64]{1,3,2,0:T(8,128)S(1)}, f32[8,2,512]{2,1,0:T(2,128)S(1)}, s32[8,512]{1,0:T(8,128)S(1)}, s32[1,4096]{1,0:T(1,128)S(1)...) while((s32[]{:T(128)}, f32[8,512,2,64]{1,3,2,0:T(8,128)S(1)}, ...), condition=%wide.region_5.6_spmd.clone.clone.clone, body=%wide.region_2.5_spmd.clone.clone.sunk.clone | while | flops 1136655872 | bytes 61275252 | solution.py:79
  268.7 45.1 %reduce-scatter.5.cloned.1.call-done = bf16[1024,512]{1,0:T(8,128)(2,1)} async-done(((bf16[4096,512]{1,0:T(8,128)(2,1)}), bf16[1024,512]{1,0:T(8,128)(2,1)}) %reduce-scatter.5.cloned.1.call-update) | async-done | bytes 1048592 | tf_op jit(solution)/shard_map/reduce_scatter | solution.py:199
  320.4 33.5 %all_gather.29 = bf16[512,512]{1,0:T(8,128)(2,1)} all-gather(bf16[64,512]{1,0:T(8,128)(2,1)S(1)} %copy-done.26), channel_id=1, replica_groups=mesh['fsdp'=8,'tp'=4] {'fsdp'}, dimensions={0}, use_global_device_ids=true | all-gather | bytes 589824 | tf_op jit(solution)/shard_map/all_gather | solution.py:164
  354.0 33.5 %all_gather.30 = bf16[512,512]{0,1:T(8,128)(2,1)} all-gather(bf16[512,64]{0,1:T(8,128)(2,1)S(1)} %copy-done.27), channel_id=1, replica_groups=mesh['fsdp'=8,'tp'=4] {'fsdp'}, dimensions={1}, use_global_device_ids=true | all-gather | bytes 589824 | tf_op jit(solution)/shard_map/all_gather | solution.py:165
  387.5 10.4 %multiply_convert_fusion.2 = (bf16[4096,512]{1,0:T(8,128)(2,1)}, f32[4096,512]{1,0:T(8,128)}) fusion(f32[512]{0:T(512)S(1)} %dynamic-slice_convert_fusion, bf16[4096,512]{1,0:T(8,128)(2,1)} %all-gather.6.cloned.1.call-done, bf16[512,512]{1,0:T(8,128)(2,1)} %all_gather.29), kind=kOutput, calls=%fused_computation.66 | convolution fusion | flops 2162163712 | bytes 17303552 | tf_op jit(solution)/shard_map/dot_general | solution.py:212
  397.9 9.8 convert_reduce_fusion
  421.6 37.4 %reduce-scatter.9.cloned.1.call-done = bf16[1024,512]{1,0:T(8,128)(2,1)} async-done(((bf16[4096,512]{1,0:T(8,128)(2,1)}), bf16[1024,512]{1,0:T(8,128)(2,1)}) %reduce-scatter.9.cloned.1.call-update) | async-done | bytes 1048592 | tf_op jit(solution)/shard_map/reduce_scatter | solution.py:231
  462.3 43.7 %reduce-scatter.7.cloned.1.call-done = bf16[1024,512]{1,0:T(8,128)(2,1)} async-done(((bf16[4096,512]{1,0:T(8,128)(2,1)}), bf16[1024,512]{1,0:T(8,128)(2,1)}) %reduce-scatter.7.cloned.1.call-update) | async-done | bytes 1048592 | tf_op jit(solution)/shard_map/reduce_scatter | solution.py:217
  511.7 14.2 %collective-permute-done = bf16[1024,512]{1,0:T(8,128)(2,1)S(1)} collective-permute-done((bf16[1024,512]{1,0:T(8,128)(2,1)S(1)}, bf16[1024,512]{1,0:T(8,128)(2,1)S(1)}, u32[]{:S(2)}, u32[]{:S(2)}) %collective-permute-start) | collective-permute-done | bytes 1048608 | tf_op jit(solution)/shard_map/ppermute | solution.py:254
  526.8 14.3 %collective-permute-done.1 = bf16[1024,512]{1,0:T(8,128)(2,1)} collective-permute-done((bf16[1024,512]{1,0:T(8,128)(2,1)S(1)}, bf16[1024,512]{1,0:T(8,128)(2,1)}, u32[]{:S(2)}, u32[]{:S(2)}) %collective-permute-start.1) | collective-permute-done | bytes 1048608 | tf_op jit(solution)/shard_map/ppermute | solution.py:254
  542.9 12.8 %collective-permute-done.2 = bf16[1024,512]{1,0:T(8,128)(2,1)} collective-permute-done((bf16[1024,512]{1,0:T(8,128)(2,1)}, bf16[1024,512]{1,0:T(8,128)(2,1)}, u32[]{:S(2)}, u32[]{:S(2)}) %collective-permute-start.2) | collective-permute-done | bytes 1048608 | tf_op jit(solution)/shard_map/ppermute | solution.py:254
  575.5 300.8 %while.33 = (s32[]{:T(128)}, f32[4096,2,64]{0,2,1:T(8,128)S(1)}, f32[4096,2,64]{0,2,1:T(8,128)}, bf16[8,512,2,64]{1,3,2,0:T(8,128)(2,1)}, bf16[8,512,2,64]{1,3,2...) while((s32[]{:T(128)}, f32[4096,2,64]{0,2,1:T(8,128)S(1)}, ...), condition=%wide.region_15.16_spmd.clone.clone.clone, body=%wide.region_14.15_spmd.clone.clone.sunk.clone | while | flops 2745172480 | bytes 161287376 | solution.py:128
  596.3 10.5 %multiply_convert_fusion.8 = bf16[2,512,4096]{2,1,0:T(8,128)(2,1)S(1)} fusion(f32[2,512,4096]{2,1,0:T(8,128)} %copy-done, bf16[4096,2,64]{0,2,1:T(8,128)(2,1)} %get-tuple-element.648, f32[2,512]{1,0:T(2,128)S(1)} %bitcast.229, f32[2,512]{1,0:T(2,128)S(1)} %dynamic-slice_bitcast_fusion.3, pred[512,4096]{1,0:T(8,128)(4,1)S(1)} %fusion.171, ...), kind=kOutput, calls=%fused_computation.26.clone.1.clone | convolution fusion | flops 566231040 | bytes 28450820 | tf_op jit(solution)/shard_map/while/body/eval_jaxpr/qhe,khe->hqk/dot_general | solution.py:107
  633.9 10.5 %multiply_convert_fusion.8 = bf16[2,512,4096]{2,1,0:T(8,128)(2,1)S(1)} fusion(f32[2,512,4096]{2,1,0:T(8,128)} %copy-done, bf16[4096,2,64]{0,2,1:T(8,128)(2,1)} %get-tuple-element.648, f32[2,512]{1,0:T(2,128)S(1)} %bitcast.229, f32[2,512]{1,0:T(2,128)S(1)} %dynamic-slice_bitcast_fusion.3, pred[512,4096]{1,0:T(8,128)(4,1)S(1)} %fusion.171, ...), kind=kOutput, calls=%fused_computation.26.clone.1.clone | convolution fusion | flops 566231040 | bytes 28450820 | tf_op jit(solution)/shard_map/while/body/eval_jaxpr/qhe,khe->hqk/dot_general | solution.py:107
  671.5 10.5 %multiply_convert_fusion.8 = bf16[2,512,4096]{2,1,0:T(8,128)(2,1)S(1)} fusion(f32[2,512,4096]{2,1,0:T(8,128)} %copy-done, bf16[4096,2,64]{0,2,1:T(8,128)(2,1)} %get-tuple-element.648, f32[2,512]{1,0:T(2,128)S(1)} %bitcast.229, f32[2,512]{1,0:T(2,128)S(1)} %dynamic-slice_bitcast_fusion.3, pred[512,4096]{1,0:T(8,128)(4,1)S(1)} %fusion.171, ...), kind=kOutput, calls=%fused_computation.26.clone.1.clone | convolution fusion | flops 566231040 | bytes 28450820 | tf_op jit(solution)/shard_map/while/body/eval_jaxpr/qhe,khe->hqk/dot_general | solution.py:107
  709.1 10.5 %multiply_convert_fusion.8 = bf16[2,512,4096]{2,1,0:T(8,128)(2,1)S(1)} fusion(f32[2,512,4096]{2,1,0:T(8,128)} %copy-done, bf16[4096,2,64]{0,2,1:T(8,128)(2,1)} %get-tuple-element.648, f32[2,512]{1,0:T(2,128)S(1)} %bitcast.229, f32[2,512]{1,0:T(2,128)S(1)} %dynamic-slice_bitcast_fusion.3, pred[512,4096]{1,0:T(8,128)(4,1)S(1)} %fusion.171, ...), kind=kOutput, calls=%fused_computation.26.clone.1.clone | convolution fusion | flops 566231040 | bytes 28450820 | tf_op jit(solution)/shard_map/while/body/eval_jaxpr/qhe,khe->hqk/dot_general | solution.py:107
  746.7 10.5 %multiply_convert_fusion.8 = bf16[2,512,4096]{2,1,0:T(8,128)(2,1)S(1)} fusion(f32[2,512,4096]{2,1,0:T(8,128)} %copy-done, bf16[4096,2,64]{0,2,1:T(8,128)(2,1)} %get-tuple-element.648, f32[2,512]{1,0:T(2,128)S(1)} %bitcast.229, f32[2,512]{1,0:T(2,128)S(1)} %dynamic-slice_bitcast_fusion.3, pred[512,4096]{1,0:T(8,128)(4,1)S(1)} %fusion.171, ...), kind=kOutput, calls=%fused_computation.26.clone.1.clone | convolution fusion | flops 566231040 | bytes 28450820 | tf_op jit(solution)/shard_map/while/body/eval_jaxpr/qhe,khe->hqk/dot_general | solution.py:107
  784.3 10.5 %multiply_convert_fusion.8 = bf16[2,512,4096]{2,1,0:T(8,128)(2,1)S(1)} fusion(f32[2,512,4096]{2,1,0:T(8,128)} %copy-done, bf16[4096,2,64]{0,2,1:T(8,128)(2,1)} %get-tuple-element.648, f32[2,512]{1,0:T(2,128)S(1)} %bitcast.229, f32[2,512]{1,0:T(2,128)S(1)} %dynamic-slice_bitcast_fusion.3, pred[512,4096]{1,0:T(8,128)(4,1)S(1)} %fusion.171, ...), kind=kOutput, calls=%fused_computation.26.clone.1.clone | convolution fusion | flops 566231040 | bytes 28450820 | tf_op jit(solution)/shard_map/while/body/eval_jaxpr/qhe,khe->hqk/dot_general | solution.py:107
  821.9 10.5 %multiply_convert_fusion.8 = bf16[2,512,4096]{2,1,0:T(8,128)(2,1)S(1)} fusion(f32[2,512,4096]{2,1,0:T(8,128)} %copy-done, bf16[4096,2,64]{0,2,1:T(8,128)(2,1)} %get-tuple-element.648, f32[2,512]{1,0:T(2,128)S(1)} %bitcast.229, f32[2,512]{1,0:T(2,128)S(1)} %dynamic-slice_bitcast_fusion.3, pred[512,4096]{1,0:T(8,128)(4,1)S(1)} %fusion.171, ...), kind=kOutput, calls=%fused_computation.26.clone.1.clone | convolution fusion | flops 566231040 | bytes 28450820 | tf_op jit(solution)/shard_map/while/body/eval_jaxpr/qhe,khe->hqk/dot_general | solution.py:107
  859.5 10.5 %multiply_convert_fusion.8 = bf16[2,512,4096]{2,1,0:T(8,128)(2,1)S(1)} fusion(f32[2,512,4096]{2,1,0:T(8,128)} %copy-done, bf16[4096,2,64]{0,2,1:T(8,128)(2,1)} %get-tuple-element.648, f32[2,512]{1,0:T(2,128)S(1)} %bitcast.229, f32[2,512]{1,0:T(2,128)S(1)} %dynamic-slice_bitcast_fusion.3, pred[512,4096]{1,0:T(8,128)(4,1)S(1)} %fusion.171, ...), kind=kOutput, calls=%fused_computation.26.clone.1.clone | convolution fusion | flops 566231040 | bytes 28450820 | tf_op jit(solution)/shard_map/while/body/eval_jaxpr/qhe,khe->hqk/dot_general | solution.py:107
  930.4 9.1 all-to-all-done.2
  974.8 39.5 %all-reduce = (f32[512]{0:T(512)}, f32[512]{0:T(512)}, f32[2,512]{1,0:T(2,128)}, f32[512]{0:T(512)}, f32[512]{0:T(512)}, /*index=5*/f32[512]{0:T(512)}, f32[2048]{0:T(1024)}, f32[512]{0:T(512)}) all-reduce(f32[512]{0:T(512)S(1)} %get-tuple-element.300, ...), channel_id=1, replica_groups=mesh['fsdp'=8,'tp'=4] {'fsdp','tp'}, use_global_device_ids=true, to_apply=%region_20.21 | all-reduce | flops 6144 | bytes 49152 | tf_op jit(solution)/shard_map/psum | solution.py:304
  (342 shorter events, 555.4 us)
Async XLA Ops:
  7.2 16.3 %copy-start.30 = (bf16[128,64]{0,1:T(8,128)(2,1)S(1)}, bf16[128,64]{0,1:T(8,128)(2,1)}, u32[]{:S(2)}) copy-start(bf16[128,64]{0,1:T(8,128)(2,1)} %param.26) | copy-start | bytes 49156
  7.2 49.6 %copy-start.28 = (bf16[64,3,128]{2,0,1:T(8,128)(2,1)S(1)}, bf16[64,3,128]{2,0,1:T(8,128)(2,1)}, u32[]{:S(2)}) copy-start(bf16[64,3,128]{2,0,1:T(8,128)(2,1)} %param.24) | copy-start | bytes 147460
  7.2 81.2 %all-gather.4.cloned.1.call-start = ((), (), s32[]{:S(2)}) async-start(), calls=%async_computation.8 | async-start | bytes 5242880 | tf_op jit(solution)/shard_map/all_gather | solution.py:177
  15.1 298.8 %reduce-scatter.5.cloned.1.call-start = ((), (), s32[]{:S(2)}) async-start(), calls=%async_computation.9 | async-start | bytes 5242880 | tf_op jit(solution)/shard_map/reduce_scatter | solution.py:199
  268.0 45.9 %copy-start.1 = (bf16[1024,512]{1,0:T(8,128)(2,1)S(1)}, bf16[1024,512]{1,0:T(8,128)(2,1)}, u32[]{:S(2)}) copy-start(bf16[1024,512]{1,0:T(8,128)(2,1)} %param.19) | copy-start | bytes 3145732
  268.0 119.5 %all-gather.6.cloned.1.call-start = ((), (), s32[]{:S(2)}) async-start(), calls=%async_computation.10 | async-start | bytes 5242880 | tf_op jit(solution)/shard_map/all_gather | solution.py:210
  317.4 36.6 %copy-start.27 = (bf16[512,64]{0,1:T(8,128)(2,1)S(1)}, bf16[512,64]{0,1:T(8,128)(2,1)}, u32[]{:S(2)}) copy-start(bf16[512,64]{0,1:T(8,128)(2,1)} %param.32) | copy-start | bytes 196612
  319.0 78.9 %all-gather.8.cloned.1.call-start = ((), (), s32[]{:S(2)}) async-start(), calls=%async_computation.12 | async-start | bytes 5242880 | tf_op jit(solution)/shard_map/all_gather | solution.py:223
  319.6 139.4 %reduce-scatter.9.cloned.1.call-start = ((), (), s32[]{:S(2)}) async-start(), calls=%async_computation.13 | async-start | bytes 5242880 | tf_op jit(solution)/shard_map/reduce_scatter | solution.py:231
  397.9 11.8 %copy-start.17 = (bf16[512,512]{1,0:T(8,128)(2,1)S(1)}, bf16[512,512]{1,0:T(8,128)(2,1)}, u32[]{:S(2)}) copy-start(bf16[512,512]{1,0:T(8,128)(2,1)} %all_gather.29) | copy-start | bytes 1572868
  414.2 91.8 %reduce-scatter.7.cloned.1.call-start = ((), (), s32[]{:S(2)}) async-start(), calls=%async_computation.11 | async-start | bytes 5242880 | tf_op jit(solution)/shard_map/reduce_scatter | solution.py:217
  421.0 551.3 %reduce-scatter.11.cloned.1.call-start = ((), (), s32[]{:S(2)}) async-start(), calls=%async_computation.14 | async-start | bytes 5242880 | tf_op jit(solution)/shard_map/reduce_scatter | solution.py:274
  511.7 14.2 %collective-permute-start = (bf16[1024,512]{1,0:T(8,128)(2,1)S(1)}, bf16[1024,512]{1,0:T(8,128)(2,1)S(1)}, u32[]{:S(2)}, u32[]{:S(2)}) collective-permute-start(bf16[1024,512]{1,0:T(8,128)(2,1)S(1)} %get-tuple-element.361), channel_id=1, source_target_pairs={{0,1},{1,2},{2,3},{3,0},{4,5},{5,6},{6,7},{7,4},{8,9},{9,10},{10,1... | collective-permute-start | bytes 3145736 | tf_op jit(solution)/shard_map/ppermute | solution.py:254
  526.8 14.3 %collective-permute-start.1 = (bf16[1024,512]{1,0:T(8,128)(2,1)S(1)}, bf16[1024,512]{1,0:T(8,128)(2,1)}, u32[]{:S(2)}, u32[]{:S(2)}) collective-permute-start(bf16[1024,512]{1,0:T(8,128)(2,1)S(1)} %collective-permute-done), channel_id=1, source_target_pairs={{0,1},{1,2},{2,3},{3,0},{4,5},{5,6},{6,7},{7,4},{8,9},{9,10},{10,1... | collective-permute-start | bytes 3145736 | tf_op jit(solution)/shard_map/ppermute | solution.py:254
  541.2 14.5 %collective-permute-start.2 = (bf16[1024,512]{1,0:T(8,128)(2,1)}, bf16[1024,512]{1,0:T(8,128)(2,1)}, u32[]{:S(2)}, u32[]{:S(2)}) collective-permute-start(bf16[1024,512]{1,0:T(8,128)(2,1)} %collective-permute-done.1), channel_id=1, source_target_pairs={{0,1},{1,2},{2,3},{3,0},{4,5},{5,6},{6,7},{7,4},{8,9},{9,10},{10,1... | collective-permute-start | bytes 3145736 | tf_op jit(solution)/shard_map/ppermute | solution.py:254
  903.5 18.4 %all-to-all-start.3 = ((bf16[8,512,64]{1,2,0:T(8,128)(2,1)}), bf16[8,512,64]{1,2,0:T(8,128)(2,1)}, u32[]{:S(2)}, u32[]{:S(2)}) async-start(bf16[8,512,64]{1,2,0:T(8,128)(2,1)} %bitcast.19), calls=%async_computation.7 | async-start | bytes 1048576 | tf_op jit(solution)/shard_map/all_to_all | solution.py:27
  909.0 17.1 %copy-start.6 = (f32[8,512,2,64]{1,3,2,0:T(8,128)S(1)}, f32[8,512,2,64]{1,3,2,0:T(8,128)}, u32[]{:S(2)}) copy-start(f32[8,512,2,64]{1,3,2,0:T(8,128)} %copy-done.4) | copy-start | bytes 6291460
  909.0 17.1 %copy-start.25 = (f32[8,512]{1,0:T(8,128)S(1)}, f32[8,512]{1,0:T(8,128)}, u32[]{:S(2)}) copy-start(f32[8,512]{1,0:T(8,128)} %get-tuple-element.375) | copy-start | bytes 49156
  921.9 17.5 %all-to-all-start.2 = ((bf16[8,64,512]{2,1,0:T(8,128)(2,1)}), bf16[8,64,512]{2,1,0:T(8,128)(2,1)}, u32[]{:S(2)}, u32[]{:S(2)}) async-start(bf16[8,64,512]{2,1,0:T(8,128)(2,1)} %bitcast.220), calls=%async_computation.6 | async-start | bytes 1048576 | tf_op jit(solution)/shard_map/all_to_all | solution.py:27
  930.4 18.9 %copy-start.10 = (bf16[4096,1,128]{2,0,1:T(8,128)(2,1)S(1)}, bf16[4096,1,128]{2,0,1:T(8,128)(2,1)}, u32[]{:S(2)}) copy-start(bf16[4096,1,128]{2,0,1:T(8,128)(2,1)} %copy-done.9) | copy-start | bytes 3145732
  930.4 18.9 %copy-start.11 = (bf16[4096,1,128]{2,0,1:T(8,128)(2,1)S(1)}, bf16[4096,1,128]{2,0,1:T(8,128)(2,1)}, u32[]{:S(2)}) copy-start(bf16[4096,1,128]{2,0,1:T(8,128)(2,1)} %copy.56) | copy-start | bytes 3145732
  945.2 11.3 %all-to-all-start.1 = ((bf16[8,128,64]{1,2,0:T(8,128)(2,1)}), bf16[8,128,64]{1,2,0:T(8,128)(2,1)S(1)}, u32[]{:S(2)}, u32[]{:S(2)}) async-start(bf16[8,128,64]{1,2,0:T(8,128)(2,1)} %bitcast.16), calls=%async_computation.5 | async-start | bytes 262144 | tf_op jit(solution)/shard_map/all_to_all | solution.py:27
  957.2 14.4 %all-to-all-start = ((bf16[8,64,3,128]{3,1,2,0:T(8,128)(2,1)}), bf16[8,64,3,128]{3,1,2,0:T(8,128)(2,1)S(1)}, u32[]{:S(2)}, u32[]{:S(2)}) async-start(bf16[8,64,3,128]{3,1,2,0:T(8,128)(2,1)} %copy.58), calls=%async_computation.4 | async-start | bytes 786432 | tf_op jit(solution)/shard_map/all_to_all | solution.py:27
  962.9 51.3 %copy-start.7 = (f32[1024,512]{1,0:T(8,128)S(1)}, f32[1024,512]{1,0:T(8,128)}, u32[]{:S(2)}) copy-start(f32[1024,512]{1,0:T(8,128)} %get-tuple-element.362) | copy-start | bytes 6291460
  (36 other events, 138.3 us)
Sparse Core Ops, SparseCore 0:
  15.2 37.1 all-gather.3
  268.1 45.6 reduce-scatter.4
  319.1 34.4 all-gather.5
  355.1 34.4 all-gather.7
  414.3 44.6 reduce-scatter.8
  461.4 44.5 reduce-scatter.6
  897.0 44.5 reduce-scatter.10
